TPU v7x, 32 devices: a whole 2x2x4 slice. The times are simulated.
32 devices in a mesh: groups: 1, row: 16 (over z, y, core), col: 2 (over x).
Axes of the slice: x: 2, y: 2, z: 4, core: 2. Of those that a mesh axis runs over, the one named last changes fastest.
Arguments:
- pair_grid: bfloat16 [256, 256, 128], P(('groups', 'row'), 'col'), may hold values from -6 to 6
- alignment_pool: bfloat16 [256, 256, 64], P('groups', 'row'), may hold values from -6 to 6
- sample_index: int32 [64], P('groups'), may hold values from 0 to 255
- token_mask: int32 [256], P('groups'), may hold values 0 or 1
- outer_proj: bfloat16 [64, 64], replicated, may hold values from -0.75 to 0.75
- outer_mix: bfloat16 [1024, 128], replicated, may hold values from -0.375 to 0.375
- pair_logit: bfloat16 [128, 8], replicated, may hold values from -1 to 1
- average_proj: bfloat16 [64, 512], replicated, may hold values from -0.75 to 0.75
- average_mix: bfloat16 [256, 64], replicated, may hold values from -0.75 to 0.75
- triangle_proj: bfloat16 [128, 640], replicated, may hold values from -0.5 to 0.5
- triangle_mix: bfloat16 [128, 128], replicated, may hold values from -0.5 to 0.5
- transition_up: bfloat16 [128, 1024], replicated, may hold values from -0.5 to 0.5
- transition_down: bfloat16 [512, 128], replicated, may hold values from -0.25 to 0.25
Outputs:
- pair_next: bfloat16 [256, 256, 128], P(('groups', 'row'), 'col')
- alignment_next: bfloat16 [64, 256, 64], P('groups', 'row')
Inputs may be any that keep to these rules, and one draw needn't show every extreme that they name: `sample_index`: indices into the first dimension of alignment_pool; they may repeat. `token_mask`: 1 marks a real residue, 0 a padded one.
All inputs are finite; a program needn't handle non-finite values.
Results may differ from a plain program's by a relative error of at most 0.008.
Values may be sent and summed in bfloat16 or wider, within the bound.
A program may use at most 64 MiB of HBM per device.

v0:
```python
import jax
import jax.numpy as jnp
from jax import lax
from jax.sharding import PartitionSpec as P

epsilon = 1e-05


def normalize(values, channel_dim):
    values = values.astype(jnp.float32)
    centred = values - jnp.mean(values, axis=channel_dim, keepdims=True)
    spread = jnp.mean(centred * centred, axis=channel_dim, keepdims=True)
    return centred / jnp.sqrt(spread + epsilon)


def triangle_product(exchanged, n_row, n_col):
    left_part = exchanged[0]
    right_part = exchanged[1]
    item_count = left_part.shape[2]
    tok_row = left_part.shape[3]
    tok_col = left_part.shape[4]
    product = jnp.einsum(
        "ruxiq,suxjq->xrisj", left_part, right_part, preferred_element_type=jnp.float32
    )
    product = product.reshape(item_count, n_row, tok_row, n_col, tok_col)
    return product.transpose(1, 3, 0, 2, 4).astype(jnp.bfloat16)


def on_device(
    pair_grid,
    alignment_pool,
    sample_index,
    token_mask,
    outer_proj,
    outer_mix,
    pair_logit,
    average_proj,
    average_mix,
    triangle_proj,
    triangle_mix,
    transition_up,
    transition_down,
):
    n_row = lax.axis_size("row")
    n_col = lax.axis_size("col")
    tok_row = pair_grid.shape[0]
    tok_col = pair_grid.shape[1]
    pair_width = pair_grid.shape[2]
    samples = sample_index.shape[0]
    align_width = alignment_pool.shape[2]
    outer_width = outer_proj.shape[1] // 2
    head_count = pair_logit.shape[1]
    head_total = average_proj.shape[1] // 2
    head_dim = head_total // head_count
    inner_width = transition_down.shape[0]
    row_start = lax.axis_index("row") * tok_row
    column_start = lax.axis_index("col") * tok_col
    alignments = jnp.take(alignment_pool, sample_index, axis=0)
    align_norm = normalize(alignments, 2).astype(jnp.bfloat16)
    align_rows = align_norm.reshape(samples, tok_row * align_width)
    gathered = lax.all_gather(align_rows, "row", axis=1, tiled=True)
    column_flat = lax.dynamic_slice_in_dim(
        gathered, column_start * align_width, tok_col * align_width, 1
    )
    column_norm = column_flat.reshape(samples, tok_col, align_width)
    row_factor = jnp.dot(
        align_norm, outer_proj[:, :outer_width], preferred_element_type=jnp.float32
    ).astype(jnp.bfloat16)
    column_factor = jnp.dot(
        column_norm, outer_proj[:, outer_width:], preferred_element_type=jnp.float32
    ).astype(jnp.bfloat16)
    column_rows = column_factor.reshape(samples, tok_col * outer_width)
    block_rows = 8
    block_count = tok_row // block_rows
    row_blocks = row_factor.reshape(samples, block_count, block_rows * outer_width).transpose(
        1, 0, 2
    )
    pair_blocks = pair_grid.reshape(block_count, block_rows, tok_col, pair_width)

    def outer_step(operands):
        left_block, pair_block = operands
        outer_sum = lax.dot_general(
            left_block, column_rows, (((0,), (0,)), ((), ())), preferred_element_type=jnp.float32
        )
        outer_sum = outer_sum.reshape(block_rows, outer_width, tok_col, outer_width).transpose(
            0, 2, 1, 3
        )
        outer_mean = (
            (outer_sum * (1.0 / samples))
            .astype(jnp.bfloat16)
            .reshape(block_rows * tok_col, outer_width * outer_width)
        )
        update = jnp.dot(outer_mean, outer_mix, preferred_element_type=jnp.float32).reshape(
            block_rows, tok_col, pair_width
        )
        return (pair_block.astype(jnp.float32) + update).astype(jnp.bfloat16)

    pair_one = lax.map(outer_step, (row_blocks, pair_blocks)).reshape(tok_row, tok_col, pair_width)
    pair_norm = normalize(pair_one, 2).astype(jnp.bfloat16)
    value_weight = average_proj[:, :head_total].reshape(align_width, head_count, head_dim)
    gate_weight = average_proj[:, head_total:].reshape(align_width, head_count, head_dim)
    mix_weight = average_mix.reshape(head_count, head_dim, align_width)
    scores = lax.dot_general(
        pair_logit, pair_norm, (((0,), (2,)), ((), ())), preferred_element_type=jnp.float32
    )
    weights = jnp.exp(scores)
    partial_total = jnp.sum(weights, axis=2)
    weights_low = weights.astype(jnp.bfloat16)
    column_values = jnp.einsum(
        "sjm,mhc->hjsc", column_norm, value_weight, preferred_element_type=jnp.float32
    )
    column_values = column_values.astype(jnp.bfloat16).reshape(
        head_count, tok_col, samples * head_dim
    )
    partial_sum = jnp.einsum(
        "hij,hjk->hik", weights_low, column_values, preferred_element_type=jnp.float32
    )
    weighted, totals = (
        lax.psum(partial_sum.astype(jnp.bfloat16), "col").astype(jnp.float32),
        lax.psum(partial_total.astype(jnp.bfloat16), "col").astype(jnp.float32),
    )
    gate_values = jax.nn.sigmoid(
        jnp.einsum("sim,mhc->hisc", align_norm, gate_weight, preferred_element_type=jnp.float32)
    )
    weighted = weighted.reshape(head_count, tok_row, samples, head_dim)
    averaged = (gate_values * weighted / totals[:, :, None, None]).astype(jnp.bfloat16)
    align_update = jnp.einsum(
        "hisc,hcm->sim", averaged, mix_weight, preferred_element_type=jnp.float32
    )
    alignment_next = (alignments.astype(jnp.float32) + align_update).astype(jnp.bfloat16)
    flat_norm = pair_norm.reshape(tok_row * tok_col, pair_width)
    projected = lax.dot_general(
        triangle_proj[:, : 4 * pair_width],
        flat_norm,
        (((0,), (1,)), ((), ())),
        preferred_element_type=jnp.float32,
    )
    projected = projected.reshape(4, pair_width, tok_row, tok_col)
    row_mask = lax.dynamic_slice_in_dim(token_mask, row_start, tok_row, 0).astype(jnp.float32)
    column_mask = lax.dynamic_slice_in_dim(token_mask, column_start, tok_col, 0).astype(jnp.float32)
    pair_mask = row_mask[:, None] * column_mask[None, :]
    left_side = jax.nn.sigmoid(projected[0]) * projected[1] * pair_mask
    right_side = jax.nn.sigmoid(projected[2]) * projected[3] * pair_mask
    factors = jnp.stack([left_side, right_side]).astype(jnp.bfloat16)
    group_size = pair_width // (n_row * n_col)
    grouped = factors.reshape(2, n_row * n_col, group_size, tok_row, tok_col)
    received = lax.all_to_all(grouped, ("row", "col"), split_axis=1, concat_axis=1, tiled=True)
    arranged = received.reshape(2, n_row, n_col, received.shape[2], tok_row, tok_col)
    result = triangle_product(arranged, n_row, n_col)
    flat_result = result.reshape(n_row * n_col, result.shape[2], tok_row, tok_col)
    product = lax.all_to_all(flat_result, ("row", "col"), split_axis=0, concat_axis=0, tiled=True)
    product = product.reshape(pair_width, tok_row, tok_col)
    product_norm = normalize(product, 0).astype(jnp.bfloat16).reshape(pair_width, tok_row * tok_col)
    mixed = lax.dot_general(
        product_norm, triangle_mix, (((0,), (0,)), ((), ())), preferred_element_type=jnp.float32
    )
    gate_out = jax.nn.sigmoid(
        jnp.dot(flat_norm, triangle_proj[:, 4 * pair_width :], preferred_element_type=jnp.float32)
    )
    pair_two = (
        pair_one.reshape(tok_row * tok_col, pair_width).astype(jnp.float32) + gate_out * mixed
    ).astype(jnp.bfloat16)
    tail_rows = pair_two.reshape(block_count, block_rows * tok_col, pair_width)

    def transition_step(rows_block):
        normed = normalize(rows_block, 1).astype(jnp.bfloat16)
        expanded = jnp.dot(normed, transition_up, preferred_element_type=jnp.float32)
        hidden = (jax.nn.silu(expanded[:, :inner_width]) * expanded[:, inner_width:]).astype(
            jnp.bfloat16
        )
        return (
            rows_block.astype(jnp.float32)
            + jnp.dot(hidden, transition_down, preferred_element_type=jnp.float32)
        ).astype(jnp.bfloat16)

    pair_next = lax.map(transition_step, tail_rows).reshape(tok_row, tok_col, pair_width)
    return (pair_next, alignment_next)


def solution(mesh):
    in_specs = (
        P(("groups", "row"), "col", None),
        P("groups", "row", None),
        P("groups"),
        P("groups"),
        P(),
        P(),
        P(),
        P(),
        P(),
        P(),
        P(),
        P(),
        P(),
    )
    out_specs = (P(("groups", "row"), "col", None), P("groups", "row", None))
    return jax.shard_map(
        on_device, mesh=mesh, in_specs=in_specs, out_specs=out_specs, check_vma=False
    )
```

profile of v0, /device:TPU:0, one launch (start us, length us, event | category | flops | bytes accessed | tf_op | source)
XLA Modules:
  0.0 163.6 jit_solution(2614358065298384016)
XLA Ops:
  8.5 2.0 %copy.82 = bf16[256,16,64]{2,1,0:T(8,128)(2,1)S(1)} copy(bf16[256,16,64]{0,2,1:T(8,128)(2,1)} %param.18) | data formatting | bytes 1048576 | tf_op args[1]
  14.1 1.2 convolution_convert_fusion.2
  15.3 42.9 %all-gather.2.cloned.1.call-done = bf16[64,16384]{1,0:T(8,128)(2,1)} async-done(((bf16[64,1024]{1,0:T(8,128)(2,1)}), bf16[64,16384]{1,0:T(8,128)(2,1)}) %all-gather.2.cloned.1.call-update) | async-done | bytes 2097168 | tf_op jit(solution)/shard_map/all_gather | solution.py:61
  58.2 2.3 %constant_dynamic-slice_fusion.1 = bf16[64,8192]{1,0:T(8,128)(2,1)} fusion(bf16[64,16384]{1,0:T(8,128)(2,1)} %all-gather.2.cloned.1.call-done, s32[]{:T(128)S(6)} %select_n.24), kind=kLoop, calls=%fused_computation.116 | loop fusion | bytes 2097156 | tf_op jit(solution)/shard_map/dynamic_slice | solution.py:62
  60.5 3.3 %reshape.294 = bf16[64,128,64]{2,1,0:T(8,128)(2,1)S(1)} reshape(bf16[64,8192]{1,0:T(8,128)(2,1)} %constant_dynamic-slice_fusion.1) | data formatting | bytes 2097152 | tf_op jit(solution)/shard_map/reshape | solution.py:65
  63.8 1.3 copy-done.1
  65.1 0.9 convolution_convert_fusion.1
  66.0 1.7 %copy.89 = bf16[64,128,32]{0,2,1:T(8,128)(2,1)S(1)} copy(bf16[64,128,32]{1,2,0:T(8,128)(2,1)S(1)} %convolution_convert_fusion.1) | data formatting | bytes 1048576 | tf_op jit(solution)/shard_map/convert_element_type | solution.py:71
  67.7 9.3 %while.20 = (s32[]{:T(128)}, bf16[2,8,128,128]{3,2,1,0:T(8,128)(2,1)S(1)}, bf16[2,8,128,128]{3,2,1,0:T(8,128)(2,1)}, bf16[2,64,256]{1,2,0:T(8,128)(2,1)}, bf16[6...) while((s32[]{:T(128)}, bf16[2,8,128,128]{3,2,1,0:T(8,128)(2,1)S(1)}, ...), condition=%wide.region_3.4_spmd, body=%wide.region_2.3_spmd.sunk | while | flops 405143552 | bytes 13992077 | solution.py:98
  68.6 1.1 copy.148
  73.2 1.1 copy.148
  80.0 1.6 slice_multiply_fusion.2
  82.1 1.6 copy.91
  84.2 1.2 copy.92
  85.5 3.5 %all-to-all-start = ((bf16[2,32,4,16,128]{4,3,2,0,1:T(8,128)(2,1)}), bf16[2,32,4,16,128]{4,3,2,0,1:T(8,128)(2,1)}, u32[]{:S(2)}, u32[]{:S(2)}) async-start(bf16[2,32,4,16,128]{4,3,2,0,1:T(8,128)(2,1)} %copy.92), calls=%async_computation | async-start | bytes 2097152 | tf_op jit(solution)/shard_map/all_to_all | solution.py:147
  89.4 1.3 convert_bitcast_fusion.1
  92.5 1.2 convolution_convert_fusion
  93.7 1.6 %reshape.302 = bf16[8,16,64,32]{3,2,1,0:T(8,128)(2,1)S(1)} reshape(bf16[8,16,2048]{2,1,0:T(8,128)(2,1)S(1)} %convolution_convert_fusion) | data formatting | bytes 1048576 | tf_op jit(solution)/shard_map/reshape | solution.py:125
  95.3 1.6 copy.103
  97.0 18.1 %all-to-all-done = bf16[2,32,4,16,128]{4,3,2,0,1:T(8,128)(2,1)} async-done(((bf16[2,32,4,16,128]{4,3,2,0,1:T(8,128)(2,1)}), bf16[2,32,4,16,128]{4,3,2,0,1:T(8,128)(2,1)}, u32[]{:S(2)}, u32[]{:S(2)}) %all-to-all-start) | async-done | bytes 1048608 | tf_op jit(solution)/shard_map/all_to_all | solution.py:147
  115.1 1.4 fusion.76
  116.6 1.3 bitcast_convert_fusion
  117.9 3.0 %copy.95 = bf16[4,16,16,16,16]{4,3,2,1,0:T(8,128)(2,1)} copy(bf16[4,16,16,16,16]{4,2,3,1,0:T(8,128)(2,1)S(1)} %bitcast_convert_fusion) | data formatting | bytes 1048576 | tf_op jit(solution)/shard_map/convert_element_type | solution.py:26
  120.9 5.8 %convert_element_type.146 = bf16[4,16,16,2,128]{4,3,2,1,0:T(2,128)(2,1)S(1)} reshape(bf16[4,16,16,16,16]{4,3,2,1,0:T(8,128)(2,1)} %copy.95) | data formatting | bytes 1048576 | tf_op jit(solution)/shard_map/convert_element_type | solution.py:26
  126.7 0.9 copy.96
  127.7 3.6 %all-to-all-start.1 = ((bf16[32,4,16,128]{3,2,1,0:T(8,128)(2,1)}), bf16[32,4,16,128]{3,2,1,0:T(8,128)(2,1)S(1)}, u32[]{:S(2)}, u32[]{:S(2)}) async-start(bf16[32,4,16,128]{3,2,1,0:T(8,128)(2,1)} %bitcast.34), calls=%async_computation.1 | async-start | bytes 1048576 | tf_op jit(solution)/shard_map/all_to_all | solution.py:151
  131.6 8.5 %psum.15 = bf16[8,16]{1,0:T(8,128)(2,1)S(1)} all-reduce(bf16[8,16]{1,0:T(8,128)(2,1)S(1)} %copy.104), channel_id=1, replica_groups=mesh['groups'=1,'row'=16,'col'=2] {'col'}, use_global_device_ids=true, to_apply=%region_14.15 | all-reduce | flops 128 | bytes 512 | tf_op jit(solution)/shard_map/psum | solution.py:120
  140.2 2.1 %fusion.26 = f32[2048,128]{1,0:T(8,128)} fusion(bf16[2048,128]{1,0:T(8,128)(2,1)S(1)} %copy-done.5, bf16[128,640]{1,0:T(8,128)(2,1)} %param.26), kind=kOutput, calls=%fused_computation.39 | convolution fusion | flops 67895296 | bytes 1605632 | tf_op jit(solution)/shard_map/dot_general | solution.py:158
  142.3 3.7 %all-reduce.2.cloned.1.call-done = bf16[8,16,64,32]{2,3,1,0:T(8,128)(2,1)} async-done(((bf16[8,16,64,32]{2,3,1,0:T(8,128)(2,1)}), bf16[8,16,64,32]{2,3,1,0:T(8,128)(2,1)}) %all-reduce.2.cloned.1.call-update) | async-done | bytes 524304 | tf_op jit(solution)/shard_map/psum | solution.py:119
  146.1 2.5 %fusion.32 = bf16[64,16,64]{2,0,1:T(8,128)(2,1)S(1)} fusion(bf16[8,32,64,1]{2,1,3,0:T(8,128)(2,1)S(1)} %bitcast.239, bf16[8,16,64,32]{2,3,1,0:T(8,128)(2,1)} %all-reduce.2.cloned.1.call-done, bf16[64,8,32,1]{0,2,3,1:T(8,128)(2,1)S(1)} %bitcast.238, f32[8,16]{1,0:T(8,128)S(1)} %convert_element_type.161, f32[64,16]{0,1:T(8,128)S(1)} %add_sqrt_fusion.2, ...), kind=kOutput, calls=%fused_computation.49 | convolution fusion | flops 69533696 | bytes 860736 | tf_op jit(solution)/shard_map/hisc,hcm->sim/dot_general | solution.py:127
  149.9 1.8 %fusion.27 = bf16[2048,128]{1,0:T(8,128)(2,1)S(1)} fusion(f32[2048,128]{1,0:T(8,128)} %fusion.26, bf16[128,128]{1,0:T(8,128)(2,1)S(1)} %copy-done, f32[16,8,16,128]{3,2,1,0:T(8,128)S(1)} %bitcast_convert_fusion.1, f32[2048]{0:T(1024)S(1)} %sqrt_bitcast_fusion, f32[2048]{0:T(1024)S(1)} %get-tuple-element.106, bf16[2048,128]{1,0:T(8,128)(2,1)S(1)} %bitcast.227), kind=kOutput, calls=%fused_computation.41 | convolution fusion | flops 68943872 | bytes 3194880 | tf_op jit(solution)/shard_map/dot_general | solution.py:154
  151.8 4.2 %while.21 = (s32[]{:T(128)}, bf16[2,1024,128]{2,1,0:T(8,128)(2,1)S(1)}, bf16[2,1024,128]{2,1,0:T(8,128)(2,1)S(1)}, bf16[128,1024]{1,0:T(8,128)(2,1)S(1)}, bf16[512,128]{1,0:T(8,128)(2,1)S(1)}, /*index=5*/s32[]{:T(128)}) while((s32[]{:T(128)}, bf16[2,1024,128]{2,1,0:T(8,128)(2,1)S(1)}, bf16[2,1024,128]{2,1,0:T(8,128)(2,1)S(1)}, ...), condition=%wide.region_11.12_spmd, body=%wide.region_8.11_spmd.sunk | while | flops 407503872 | bytes 10129493 | solution.py:176
  (109 shorter events, 24.8 us)
Async XLA Ops:
  7.2 142.7 %copy-start = (bf16[128,128]{1,0:T(8,128)(2,1)S(1)}, bf16[128,128]{1,0:T(8,128)(2,1)}, u32[]{:S(2)}) copy-start(bf16[128,128]{1,0:T(8,128)(2,1)} %param.27) | copy-start | bytes 98308
  7.2 51.0 %all-gather.2.cloned.1.call-start = ((), (), s32[]{:S(2)}) async-start(), calls=%async_computation.2 | async-start | bytes 2228224 | tf_op jit(solution)/shard_map/all_gather | solution.py:61
  11.9 2.0 %copy-start.14 = (s32[256]{0:T(256)S(1)}, s32[256]{0:T(256)}, u32[]{:S(2)}) copy-start(s32[256]{0:T(256)} %param.20) | copy-start | bytes 3076
  11.9 2.2 %copy-start.9 = (bf16[64,64]{1,0:T(8,128)(2,1)S(1)}, bf16[64,64]{1,0:T(8,128)(2,1)}, u32[]{:S(2)}) copy-start(bf16[64,64]{1,0:T(8,128)(2,1)} %param.21) | copy-start | bytes 24580
  63.8 1.3 copy-start.1
  70.4 1.0 copy-start.11
  70.4 1.1 copy-start.12
  75.0 1.0 copy-start.11
  75.0 1.1 copy-start.12
  77.0 2.3 %copy-start.6 = (bf16[128,640]{1,0:T(8,128)(2,1)S(1)}, bf16[128,640]{1,0:T(8,128)(2,1)}, u32[]{:S(2)}) copy-start(bf16[128,640]{1,0:T(8,128)(2,1)} %param.26) | copy-start | bytes 491524
  78.5 0.8 copy-start.4
  84.2 5.0 %copy-start.7 = (bf16[64,512]{1,0:T(8,128)(2,1)S(1)}, bf16[64,512]{1,0:T(8,128)(2,1)}, u32[]{:S(2)}) copy-start(bf16[64,512]{1,0:T(8,128)(2,1)} %param.24) | copy-start | bytes 196612
  84.2 5.1 %copy-start.2 = (bf16[64,128,64]{2,1,0:T(8,128)(2,1)S(1)}, bf16[64,128,64]{2,1,0:T(8,128)(2,1)}, u32[]{:S(2)}) copy-start(bf16[64,128,64]{2,1,0:T(8,128)(2,1)} %copy-done.1) | copy-start | bytes 3145732
  85.5 29.6 %all-to-all-start = ((bf16[2,32,4,16,128]{4,3,2,0,1:T(8,128)(2,1)}), bf16[2,32,4,16,128]{4,3,2,0,1:T(8,128)(2,1)}, u32[]{:S(2)}, u32[]{:S(2)}) async-start(bf16[2,32,4,16,128]{4,3,2,0,1:T(8,128)(2,1)} %copy.92), calls=%async_computation | async-start | bytes 2097152 | tf_op jit(solution)/shard_map/all_to_all | solution.py:147
  88.9 57.1 %all-reduce.2.cloned.1.call-start = ((), (), s32[]{:S(2)}) async-start(), calls=%async_computation.3 | async-start | bytes 2097152 | tf_op jit(solution)/shard_map/psum | solution.py:119
  90.6 1.5 copy-start.10
  126.7 4.7 %copy-start.8 = (bf16[256,64]{0,1:T(8,128)(2,1)S(1)}, bf16[256,64]{0,1:T(8,128)(2,1)}, u32[]{:S(2)}) copy-start(bf16[256,64]{0,1:T(8,128)(2,1)} %param.25) | copy-start | bytes 98308
  126.7 13.5 %copy-start.5 = (bf16[2048,128]{1,0:T(8,128)(2,1)S(1)}, bf16[2048,128]{1,0:T(8,128)(2,1)}, u32[]{:S(2)}) copy-start(bf16[2048,128]{1,0:T(8,128)(2,1)} %copy-done.4) | copy-start | bytes 1572868
  127.7 21.7 %all-to-all-start.1 = ((bf16[32,4,16,128]{3,2,1,0:T(8,128)(2,1)}), bf16[32,4,16,128]{3,2,1,0:T(8,128)(2,1)S(1)}, u32[]{:S(2)}, u32[]{:S(2)}) async-start(bf16[32,4,16,128]{3,2,1,0:T(8,128)(2,1)} %bitcast.34), calls=%async_computation.1 | async-start | bytes 1048576 | tf_op jit(solution)/shard_map/all_to_all | solution.py:151
  149.9 1.8 %copy-start.3 = (bf16[128,1024]{1,0:T(8,128)(2,1)S(1)}, bf16[128,1024]{1,0:T(8,128)(2,1)}, u32[]{:S(2)}) copy-start(bf16[128,1024]{1,0:T(8,128)(2,1)} %param.28) | copy-start | bytes 786436
  149.9 1.8 %copy-start.13 = (bf16[512,128]{1,0:T(8,128)(2,1)S(1)}, bf16[512,128]{1,0:T(8,128)(2,1)}, u32[]{:S(2)}) copy-start(bf16[512,128]{1,0:T(8,128)(2,1)} %param.29) | copy-start | bytes 393220
  156.0 0.8 copy-start.15
Sparse Core Ops, SparseCore 0:
  14.0 44.1 all-gather.1
  97.1 48.9 all-reduce.1
where the time goes:
time: 165 us; the launch traced here: 164 us
  waiting for transfers between devices  64.8 us (39%)
  local copies, waits for them, and re-layouts  40.2 us (24%)
  matrix products  19.4 us (12%)
  between operations  14.5 us (9%)
  blocking collectives  8.55 us (5%)
  other arithmetic  8.53 us (5%)
  starting transfers between devices  7.4 us (4%)
    all_gather x1, waiting for transfers between devices, on_device(): gathered = lax.all_gather(align_rows, 'row', axis=1, tiled=True)  42.9 us
    all_to_all x1, waiting for transfers between devices, on_device(): lax.all_to_all(grouped, ('row', 'col'), split_axis=1, concat_axis=1, tile...  18.1 us
    convert_element_type x3, local copies, waits for them, and re-layouts, triangle_product(): return product.transpose(1, 3, 0, 2, 4).astype(jnp.bfloat16)  9.76 us
    psum x1, blocking collectives, on_device(): lax.psum(partial_total.astype(jnp.bfloat16), 'col').astype(jnp.float32)  8.55 us
    unnamed x36, local copies, waits for them, and re-layouts  6.61 us
    psum x1, waiting for transfers between devices, on_device(): lax.psum(partial_sum.astype(jnp.bfloat16), 'col').astype(jnp.float32)  3.71 us
    all_to_all x1, starting transfers between devices, on_device(): lax.all_to_all(flat_result, ('row', 'col'), split_axis=0, concat_axis=0,...  3.64 us
    all_to_all x1, starting transfers between devices, on_device(): lax.all_to_all(grouped, ('row', 'col'), split_axis=1, concat_axis=1, tile...  3.46 us
  transfers between devices with their start and end apart: 4, of which 3 were waited for; matrix products, arithmetic and copies ran while one was open for 17% of the time, Pallas kernels for 0%

commit v1 on v0

--- a/solution.py
+++ b/solution.py
@@ -58,7 +58,12 @@
     alignments = jnp.take(alignment_pool, sample_index, axis=0)
     align_norm = normalize(alignments, 2).astype(jnp.bfloat16)
     align_rows = align_norm.reshape(samples, tok_row * align_width)
-    gathered = lax.all_gather(align_rows, "row", axis=1, tiled=True)
+    ring = [align_rows]
+    for hop in range(15):
+        ring.append(lax.ppermute(ring[-1], "row", [(dev, (dev + 1) % 16) for dev in range(16)]))
+    gathered = jnp.roll(
+        jnp.concatenate(ring[::-1], axis=1), (lax.axis_index("row") + 1) * ring[0].shape[1], axis=1
+    )
     column_flat = lax.dynamic_slice_in_dim(
         gathered, column_start * align_width, tok_col * align_width, 1
     )

time: 165 us -> 228 us (1.38)
  waiting for transfers between devices: 64.8 us -> 127 us
    ppermute x0 -> x15, waiting for transfers between devices: none -> 105 us  [on_device(): lax.ppermute(ring[-1], 'row', [(dev, (dev + 1) % 16) for dev in range(16)])]
    all_gather x1 -> x0, waiting for transfers between devices: 42.9 us -> none  [on_device(): gathered = lax.all_gather(align_rows, 'row', axis=1, tiled=True)]
    unnamed x36 -> x67, local copies, waits for them, and re-layouts: 6.61 us -> 7.92 us
  transfers between devices with their start and end apart: 4 -> 18, of which waited for: 3 -> 17; matrix products, arithmetic and copies ran while one was open for 17% -> 12% of each run, Pallas kernels for 0% -> 0%
where the time goes in v1:
time: 228 us; the launch traced here: 227 us
  waiting for transfers between devices  127 us (56%)
  local copies, waits for them, and re-layouts  40.2 us (18%)
  matrix products  19.4 us (9%)
  between operations  14.8 us (6%)
  other arithmetic  9.22 us (4%)
  blocking collectives  8.54 us (4%)
  starting transfers between devices  7.78 us (3%)
    ppermute x15, waiting for transfers between devices, on_device(): lax.ppermute(ring[-1], 'row', [(dev, (dev + 1) % 16) for dev in range(16)])  105 us
    all_to_all x1, waiting for transfers between devices, on_device(): lax.all_to_all(grouped, ('row', 'col'), split_axis=1, concat_axis=1, tile...  18.1 us
    convert_element_type x3, local copies, waits for them, and re-layouts, triangle_product(): return product.transpose(1, 3, 0, 2, 4).astype(jnp.bfloat16)  9.85 us
    psum x1, blocking collectives, on_device(): lax.psum(partial_total.astype(jnp.bfloat16), 'col').astype(jnp.float32)  8.54 us
    unnamed x67, local copies, waits for them, and re-layouts  7.92 us
  transfers between devices with their start and end apart: 18, of which 17 were waited for; matrix products, arithmetic and copies ran while one was open for 12% of the time, Pallas kernels for 0%

profile of v1, /device:TPU:0, one launch (start us, length us, event | category | flops | bytes accessed | tf_op | source)
XLA Modules:
  0.0 227.4 jit_solution(2968636050808624985)
XLA Ops:
  8.5 2.0 copy.82
  13.7 7.6 %collective-permute-done = bf16[64,1024]{1,0:T(8,128)(2,1)S(1)} collective-permute-done((bf16[64,1024]{1,0:T(8,128)(2,1)S(1)}, bf16[64,1024]{1,0:T(8,128)(2,1)S(1)}, u32[]{:S(2)}, u32[]{:S(2)}) %collective-permute-start) | collective-permute-done | bytes 131104 | tf_op jit(solution)/shard_map/ppermute | solution.py:63
  21.3 7.1 %collective-permute-done.1 = bf16[64,1024]{1,0:T(8,128)(2,1)S(1)} collective-permute-done((bf16[64,1024]{1,0:T(8,128)(2,1)S(1)}, bf16[64,1024]{1,0:T(8,128)(2,1)S(1)}, u32[]{:S(2)}, u32[]{:S(2)}) %collective-permute-start.1) | collective-permute-done | bytes 131104 | tf_op jit(solution)/shard_map/ppermute | solution.py:63
  28.4 7.1 %collective-permute-done.2 = bf16[64,1024]{1,0:T(8,128)(2,1)S(1)} collective-permute-done((bf16[64,1024]{1,0:T(8,128)(2,1)S(1)}, bf16[64,1024]{1,0:T(8,128)(2,1)S(1)}, u32[]{:S(2)}, u32[]{:S(2)}) %collective-permute-start.2) | collective-permute-done | bytes 131104 | tf_op jit(solution)/shard_map/ppermute | solution.py:63
  35.5 7.1 %collective-permute-done.3 = bf16[64,1024]{1,0:T(8,128)(2,1)S(1)} collective-permute-done((bf16[64,1024]{1,0:T(8,128)(2,1)S(1)}, bf16[64,1024]{1,0:T(8,128)(2,1)S(1)}, u32[]{:S(2)}, u32[]{:S(2)}) %collective-permute-start.3) | collective-permute-done | bytes 131104 | tf_op jit(solution)/shard_map/ppermute | solution.py:63
  42.6 7.1 %collective-permute-done.4 = bf16[64,1024]{1,0:T(8,128)(2,1)S(1)} collective-permute-done((bf16[64,1024]{1,0:T(8,128)(2,1)S(1)}, bf16[64,1024]{1,0:T(8,128)(2,1)S(1)}, u32[]{:S(2)}, u32[]{:S(2)}) %collective-permute-start.4) | collective-permute-done | bytes 131104 | tf_op jit(solution)/shard_map/ppermute | solution.py:63
  49.7 7.1 %collective-permute-done.5 = bf16[64,1024]{1,0:T(8,128)(2,1)S(1)} collective-permute-done((bf16[64,1024]{1,0:T(8,128)(2,1)S(1)}, bf16[64,1024]{1,0:T(8,128)(2,1)S(1)}, u32[]{:S(2)}, u32[]{:S(2)}) %collective-permute-start.5) | collective-permute-done | bytes 131104 | tf_op jit(solution)/shard_map/ppermute | solution.py:63
  56.8 7.1 %collective-permute-done.6 = bf16[64,1024]{1,0:T(8,128)(2,1)S(1)} collective-permute-done((bf16[64,1024]{1,0:T(8,128)(2,1)S(1)}, bf16[64,1024]{1,0:T(8,128)(2,1)S(1)}, u32[]{:S(2)}, u32[]{:S(2)}) %collective-permute-start.6) | collective-permute-done | bytes 131104 | tf_op jit(solution)/shard_map/ppermute | solution.py:63
  63.9 7.1 %collective-permute-done.7 = bf16[64,1024]{1,0:T(8,128)(2,1)S(1)} collective-permute-done((bf16[64,1024]{1,0:T(8,128)(2,1)S(1)}, bf16[64,1024]{1,0:T(8,128)(2,1)S(1)}, u32[]{:S(2)}, u32[]{:S(2)}) %collective-permute-start.7) | collective-permute-done | bytes 131104 | tf_op jit(solution)/shard_map/ppermute | solution.py:63
  71.0 7.1 %collective-permute-done.8 = bf16[64,1024]{1,0:T(8,128)(2,1)S(1)} collective-permute-done((bf16[64,1024]{1,0:T(8,128)(2,1)S(1)}, bf16[64,1024]{1,0:T(8,128)(2,1)S(1)}, u32[]{:S(2)}, u32[]{:S(2)}) %collective-permute-start.8) | collective-permute-done | bytes 131104 | tf_op jit(solution)/shard_map/ppermute | solution.py:63
  78.1 7.1 %collective-permute-done.9 = bf16[64,1024]{1,0:T(8,128)(2,1)S(1)} collective-permute-done((bf16[64,1024]{1,0:T(8,128)(2,1)S(1)}, bf16[64,1024]{1,0:T(8,128)(2,1)S(1)}, u32[]{:S(2)}, u32[]{:S(2)}) %collective-permute-start.9) | collective-permute-done | bytes 131104 | tf_op jit(solution)/shard_map/ppermute | solution.py:63
  85.1 7.1 %collective-permute-done.10 = bf16[64,1024]{1,0:T(8,128)(2,1)S(1)} collective-permute-done((bf16[64,1024]{1,0:T(8,128)(2,1)S(1)}, bf16[64,1024]{1,0:T(8,128)(2,1)S(1)}, u32[]{:S(2)}, u32[]{:S(2)}) %collective-permute-start.10) | collective-permute-done | bytes 131104 | tf_op jit(solution)/shard_map/ppermute | solution.py:63
  92.2 7.1 %collective-permute-done.11 = bf16[64,1024]{1,0:T(8,128)(2,1)S(1)} collective-permute-done((bf16[64,1024]{1,0:T(8,128)(2,1)S(1)}, bf16[64,1024]{1,0:T(8,128)(2,1)S(1)}, u32[]{:S(2)}, u32[]{:S(2)}) %collective-permute-start.11) | collective-permute-done | bytes 131104 | tf_op jit(solution)/shard_map/ppermute | solution.py:63
  100.5 5.9 %collective-permute-done.12 = bf16[64,1024]{1,0:T(8,128)(2,1)S(1)} collective-permute-done((bf16[64,1024]{1,0:T(8,128)(2,1)S(1)}, bf16[64,1024]{1,0:T(8,128)(2,1)S(1)}, u32[]{:S(2)}, u32[]{:S(2)}) %collective-permute-start.12) | collective-permute-done | bytes 131104 | tf_op jit(solution)/shard_map/ppermute | solution.py:63
  106.6 6.9 %collective-permute-done.13 = bf16[64,1024]{1,0:T(8,128)(2,1)S(1)} collective-permute-done((bf16[64,1024]{1,0:T(8,128)(2,1)S(1)}, bf16[64,1024]{1,0:T(8,128)(2,1)S(1)}, u32[]{:S(2)}, u32[]{:S(2)}) %collective-permute-start.13) | collective-permute-done | bytes 131104 | tf_op jit(solution)/shard_map/ppermute | solution.py:63
  113.6 7.0 %collective-permute-done.14 = bf16[64,1024]{1,0:T(8,128)(2,1)S(1)} collective-permute-done((bf16[64,1024]{1,0:T(8,128)(2,1)S(1)}, bf16[64,1024]{1,0:T(8,128)(2,1)S(1)}, u32[]{:S(2)}, u32[]{:S(2)}) %collective-permute-start.14) | collective-permute-done | bytes 131104 | tf_op jit(solution)/shard_map/ppermute | solution.py:63
  122.5 3.3 %reshape.294 = bf16[64,128,64]{2,1,0:T(8,128)(2,1)S(1)} reshape(bf16[64,8192]{1,0:T(8,128)(2,1)} %constant_dynamic-slice_fusion.1) | data formatting | bytes 2097152 | tf_op jit(solution)/shard_map/reshape | solution.py:70
  128.0 1.7 copy.89
  129.8 8.8 %while.20 = (s32[]{:T(128)}, bf16[2,8,128,128]{3,2,1,0:T(8,128)(2,1)S(1)}, bf16[2,8,128,128]{3,2,1,0:T(8,128)(2,1)}, bf16[2,64,256]{1,2,0:T(8,128)(2,1)}, bf16[6...) while((s32[]{:T(128)}, bf16[2,8,128,128]{3,2,1,0:T(8,128)(2,1)S(1)}, ...), condition=%wide.region_3.4_spmd, body=%wide.region_2.3_spmd.sunk | while | flops 405143552 | bytes 13992077 | solution.py:103
  149.4 3.4 %all-to-all-start = ((bf16[2,32,4,16,128]{4,3,2,0,1:T(8,128)(2,1)}), bf16[2,32,4,16,128]{4,3,2,0,1:T(8,128)(2,1)}, u32[]{:S(2)}, u32[]{:S(2)}) async-start(bf16[2,32,4,16,128]{4,3,2,0,1:T(8,128)(2,1)} %copy.92), calls=%async_computation | async-start | bytes 2097152 | tf_op jit(solution)/shard_map/all_to_all | solution.py:152
  157.5 1.6 reshape.302
  159.1 1.6 copy.103
  160.8 18.1 %all-to-all-done = bf16[2,32,4,16,128]{4,3,2,0,1:T(8,128)(2,1)} async-done(((bf16[2,32,4,16,128]{4,3,2,0,1:T(8,128)(2,1)}), bf16[2,32,4,16,128]{4,3,2,0,1:T(8,128)(2,1)}, u32[]{:S(2)}, u32[]{:S(2)}) %all-to-all-start) | async-done | bytes 1048608 | tf_op jit(solution)/shard_map/all_to_all | solution.py:152
  181.7 3.0 %copy.95 = bf16[4,16,16,16,16]{4,3,2,1,0:T(8,128)(2,1)} copy(bf16[4,16,16,16,16]{4,2,3,1,0:T(8,128)(2,1)S(1)} %bitcast_convert_fusion) | data formatting | bytes 1048576 | tf_op jit(solution)/shard_map/convert_element_type | solution.py:26
  184.7 5.9 %convert_element_type.146 = bf16[4,16,16,2,128]{4,3,2,1,0:T(2,128)(2,1)S(1)} reshape(bf16[4,16,16,16,16]{4,3,2,1,0:T(8,128)(2,1)} %copy.95) | data formatting | bytes 1048576 | tf_op jit(solution)/shard_map/convert_element_type | solution.py:26
  191.5 3.6 %all-to-all-start.1 = ((bf16[32,4,16,128]{3,2,1,0:T(8,128)(2,1)}), bf16[32,4,16,128]{3,2,1,0:T(8,128)(2,1)S(1)}, u32[]{:S(2)}, u32[]{:S(2)}) async-start(bf16[32,4,16,128]{3,2,1,0:T(8,128)(2,1)} %bitcast.34), calls=%async_computation.1 | async-start | bytes 1048576 | tf_op jit(solution)/shard_map/all_to_all | solution.py:156
  195.4 8.5 %psum.15 = bf16[8,16]{1,0:T(8,128)(2,1)S(1)} all-reduce(bf16[8,16]{1,0:T(8,128)(2,1)S(1)} %copy.104), channel_id=1, replica_groups=mesh['groups'=1,'row'=16,'col'=2] {'col'}, use_global_device_ids=true, to_apply=%region_14.15 | all-reduce | flops 128 | bytes 512 | tf_op jit(solution)/shard_map/psum | solution.py:125
  204.0 2.2 fusion.26
  206.1 3.7 %all-reduce.2.cloned.1.call-done = bf16[8,16,64,32]{2,3,1,0:T(8,128)(2,1)} async-done(((bf16[8,16,64,32]{2,3,1,0:T(8,128)(2,1)}), bf16[8,16,64,32]{2,3,1,0:T(8,128)(2,1)}) %all-reduce.2.cloned.1.call-update) | async-done | bytes 524304 | tf_op jit(solution)/shard_map/psum | solution.py:124
  209.8 2.5 %fusion.32 = bf16[64,16,64]{2,0,1:T(8,128)(2,1)S(1)} fusion(bf16[8,32,64,1]{2,1,3,0:T(8,128)(2,1)S(1)} %bitcast.239, bf16[8,16,64,32]{2,3,1,0:T(8,128)(2,1)} %all-reduce.2.cloned.1.call-done, bf16[64,8,32,1]{0,2,3,1:T(8,128)(2,1)S(1)} %bitcast.238, f32[8,16]{1,0:T(8,128)S(1)} %convert_element_type.161, f32[64,16]{0,1:T(8,128)S(1)} %add_sqrt_fusion.2, ...), kind=kOutput, calls=%fused_computation.49 | convolution fusion | flops 69533696 | bytes 860736 | tf_op jit(solution)/shard_map/hisc,hcm->sim/dot_general | solution.py:132
  213.7 1.8 fusion.27
  215.5 4.2 %while.21 = (s32[]{:T(128)}, bf16[2,1024,128]{2,1,0:T(8,128)(2,1)S(1)}, bf16[2,1024,128]{2,1,0:T(8,128)(2,1)S(1)}, bf16[128,1024]{1,0:T(8,128)(2,1)S(1)}, bf16[512,128]{1,0:T(8,128)(2,1)S(1)}, /*index=5*/s32[]{:T(128)}) while((s32[]{:T(128)}, bf16[2,1024,128]{2,1,0:T(8,128)(2,1)S(1)}, bf16[2,1024,128]{2,1,0:T(8,128)(2,1)S(1)}, ...), condition=%wide.region_11.12_spmd, body=%wide.region_8.11_spmd.sunk | while | flops 407503872 | bytes 10129493 | solution.py:181
  (168 shorter events, 44.2 us)
Async XLA Ops:
  7.2 206.5 %copy-start = (bf16[128,128]{1,0:T(8,128)(2,1)S(1)}, bf16[128,128]{1,0:T(8,128)(2,1)}, u32[]{:S(2)}) copy-start(bf16[128,128]{1,0:T(8,128)(2,1)} %param.27) | copy-start | bytes 98308
  7.2 92.1 %copy-start.9 = (bf16[64,64]{1,0:T(8,128)(2,1)S(1)}, bf16[64,64]{1,0:T(8,128)(2,1)}, u32[]{:S(2)}) copy-start(bf16[64,64]{1,0:T(8,128)(2,1)} %param.21) | copy-start | bytes 24580
  8.5 97.9 %copy-start.14 = (s32[256]{0:T(256)S(1)}, s32[256]{0:T(256)}, u32[]{:S(2)}) copy-start(s32[256]{0:T(256)} %param.20) | copy-start | bytes 3076
  13.1 8.2 %collective-permute-start = (bf16[64,1024]{1,0:T(8,128)(2,1)S(1)}, bf16[64,1024]{1,0:T(8,128)(2,1)S(1)}, u32[]{:S(2)}, u32[]{:S(2)}) collective-permute-start(bf16[64,1024]{1,0:T(8,128)(2,1)S(1)} %divide_convert_fusion), channel_id=1, source_target_pairs={{0,2},{2,4},{4,6},{6,8},{8,10},{10,12},{12,14},{14,16},{16,18},{18... | collective-permute-start | bytes 393224 | tf_op jit(solution)/shard_map/ppermute | solution.py:63
  21.3 7.1 %collective-permute-start.1 = (bf16[64,1024]{1,0:T(8,128)(2,1)S(1)}, bf16[64,1024]{1,0:T(8,128)(2,1)S(1)}, u32[]{:S(2)}, u32[]{:S(2)}) collective-permute-start(bf16[64,1024]{1,0:T(8,128)(2,1)S(1)} %collective-permute-done), channel_id=1, source_target_pairs={{0,2},{2,4},{4,6},{6,8},{8,10},{10,12},{12,14},{14,16},{16,18},{18... | collective-permute-start | bytes 393224 | tf_op jit(solution)/shard_map/ppermute | solution.py:63
  28.4 7.1 %collective-permute-start.2 = (bf16[64,1024]{1,0:T(8,128)(2,1)S(1)}, bf16[64,1024]{1,0:T(8,128)(2,1)S(1)}, u32[]{:S(2)}, u32[]{:S(2)}) collective-permute-start(bf16[64,1024]{1,0:T(8,128)(2,1)S(1)} %collective-permute-done.1), channel_id=1, source_target_pairs={{0,2},{2,4},{4,6},{6,8},{8,10},{10,12},{12,14},{14,16},{16,18},{18... | collective-permute-start | bytes 393224 | tf_op jit(solution)/shard_map/ppermute | solution.py:63
  35.5 7.1 %collective-permute-start.3 = (bf16[64,1024]{1,0:T(8,128)(2,1)S(1)}, bf16[64,1024]{1,0:T(8,128)(2,1)S(1)}, u32[]{:S(2)}, u32[]{:S(2)}) collective-permute-start(bf16[64,1024]{1,0:T(8,128)(2,1)S(1)} %collective-permute-done.2), channel_id=1, source_target_pairs={{0,2},{2,4},{4,6},{6,8},{8,10},{10,12},{12,14},{14,16},{16,18},{18... | collective-permute-start | bytes 393224 | tf_op jit(solution)/shard_map/ppermute | solution.py:63
  42.6 7.1 %collective-permute-start.4 = (bf16[64,1024]{1,0:T(8,128)(2,1)S(1)}, bf16[64,1024]{1,0:T(8,128)(2,1)S(1)}, u32[]{:S(2)}, u32[]{:S(2)}) collective-permute-start(bf16[64,1024]{1,0:T(8,128)(2,1)S(1)} %collective-permute-done.3), channel_id=1, source_target_pairs={{0,2},{2,4},{4,6},{6,8},{8,10},{10,12},{12,14},{14,16},{16,18},{18... | collective-permute-start | bytes 393224 | tf_op jit(solution)/shard_map/ppermute | solution.py:63
  49.7 7.1 %collective-permute-start.5 = (bf16[64,1024]{1,0:T(8,128)(2,1)S(1)}, bf16[64,1024]{1,0:T(8,128)(2,1)S(1)}, u32[]{:S(2)}, u32[]{:S(2)}) collective-permute-start(bf16[64,1024]{1,0:T(8,128)(2,1)S(1)} %collective-permute-done.4), channel_id=1, source_target_pairs={{0,2},{2,4},{4,6},{6,8},{8,10},{10,12},{12,14},{14,16},{16,18},{18... | collective-permute-start | bytes 393224 | tf_op jit(solution)/shard_map/ppermute | solution.py:63
  56.8 7.1 %collective-permute-start.6 = (bf16[64,1024]{1,0:T(8,128)(2,1)S(1)}, bf16[64,1024]{1,0:T(8,128)(2,1)S(1)}, u32[]{:S(2)}, u32[]{:S(2)}) collective-permute-start(bf16[64,1024]{1,0:T(8,128)(2,1)S(1)} %collective-permute-done.5), channel_id=1, source_target_pairs={{0,2},{2,4},{4,6},{6,8},{8,10},{10,12},{12,14},{14,16},{16,18},{18... | collective-permute-start | bytes 393224 | tf_op jit(solution)/shard_map/ppermute | solution.py:63
  63.9 7.1 %collective-permute-start.7 = (bf16[64,1024]{1,0:T(8,128)(2,1)S(1)}, bf16[64,1024]{1,0:T(8,128)(2,1)S(1)}, u32[]{:S(2)}, u32[]{:S(2)}) collective-permute-start(bf16[64,1024]{1,0:T(8,128)(2,1)S(1)} %collective-permute-done.6), channel_id=1, source_target_pairs={{0,2},{2,4},{4,6},{6,8},{8,10},{10,12},{12,14},{14,16},{16,18},{18... | collective-permute-start | bytes 393224 | tf_op jit(solution)/shard_map/ppermute | solution.py:63
  71.0 7.1 %collective-permute-start.8 = (bf16[64,1024]{1,0:T(8,128)(2,1)S(1)}, bf16[64,1024]{1,0:T(8,128)(2,1)S(1)}, u32[]{:S(2)}, u32[]{:S(2)}) collective-permute-start(bf16[64,1024]{1,0:T(8,128)(2,1)S(1)} %collective-permute-done.7), channel_id=1, source_target_pairs={{0,2},{2,4},{4,6},{6,8},{8,10},{10,12},{12,14},{14,16},{16,18},{18... | collective-permute-start | bytes 393224 | tf_op jit(solution)/shard_map/ppermute | solution.py:63
  78.1 7.1 %collective-permute-start.9 = (bf16[64,1024]{1,0:T(8,128)(2,1)S(1)}, bf16[64,1024]{1,0:T(8,128)(2,1)S(1)}, u32[]{:S(2)}, u32[]{:S(2)}) collective-permute-start(bf16[64,1024]{1,0:T(8,128)(2,1)S(1)} %collective-permute-done.8), channel_id=1, source_target_pairs={{0,2},{2,4},{4,6},{6,8},{8,10},{10,12},{12,14},{14,16},{16,18},{18... | collective-permute-start | bytes 393224 | tf_op jit(solution)/shard_map/ppermute | solution.py:63
  85.1 7.1 %collective-permute-start.10 = (bf16[64,1024]{1,0:T(8,128)(2,1)S(1)}, bf16[64,1024]{1,0:T(8,128)(2,1)S(1)}, u32[]{:S(2)}, u32[]{:S(2)}) collective-permute-start(bf16[64,1024]{1,0:T(8,128)(2,1)S(1)} %collective-permute-done.9), channel_id=1, source_target_pairs={{0,2},{2,4},{4,6},{6,8},{8,10},{10,12},{12,14},{14,16},{16,18},{18... | collective-permute-start | bytes 393224 | tf_op jit(solution)/shard_map/ppermute | solution.py:63
  92.2 7.1 %collective-permute-start.11 = (bf16[64,1024]{1,0:T(8,128)(2,1)S(1)}, bf16[64,1024]{1,0:T(8,128)(2,1)S(1)}, u32[]{:S(2)}, u32[]{:S(2)}) collective-permute-start(bf16[64,1024]{1,0:T(8,128)(2,1)S(1)} %collective-permute-done.10), channel_id=1, source_target_pairs={{0,2},{2,4},{4,6},{6,8},{8,10},{10,12},{12,14},{14,16},{16,18},{18... | collective-permute-start | bytes 393224 | tf_op jit(solution)/shard_map/ppermute | solution.py:63
  99.3 7.1 %collective-permute-start.12 = (bf16[64,1024]{1,0:T(8,128)(2,1)S(1)}, bf16[64,1024]{1,0:T(8,128)(2,1)S(1)}, u32[]{:S(2)}, u32[]{:S(2)}) collective-permute-start(bf16[64,1024]{1,0:T(8,128)(2,1)S(1)} %collective-permute-done.11), channel_id=1, source_target_pairs={{0,2},{2,4},{4,6},{6,8},{8,10},{10,12},{12,14},{14,16},{16,18},{18... | collective-permute-start | bytes 393224 | tf_op jit(solution)/shard_map/ppermute | solution.py:63
  106.4 7.1 %collective-permute-start.13 = (bf16[64,1024]{1,0:T(8,128)(2,1)S(1)}, bf16[64,1024]{1,0:T(8,128)(2,1)S(1)}, u32[]{:S(2)}, u32[]{:S(2)}) collective-permute-start(bf16[64,1024]{1,0:T(8,128)(2,1)S(1)} %collective-permute-done.12), channel_id=1, source_target_pairs={{0,2},{2,4},{4,6},{6,8},{8,10},{10,12},{12,14},{14,16},{16,18},{18... | collective-permute-start | bytes 393224 | tf_op jit(solution)/shard_map/ppermute | solution.py:63
  113.5 7.1 %collective-permute-start.14 = (bf16[64,1024]{1,0:T(8,128)(2,1)S(1)}, bf16[64,1024]{1,0:T(8,128)(2,1)S(1)}, u32[]{:S(2)}, u32[]{:S(2)}) collective-permute-start(bf16[64,1024]{1,0:T(8,128)(2,1)S(1)} %collective-permute-done.13), channel_id=1, source_target_pairs={{0,2},{2,4},{4,6},{6,8},{8,10},{10,12},{12,14},{14,16},{16,18},{18... | collective-permute-start | bytes 393224 | tf_op jit(solution)/shard_map/ppermute | solution.py:63
  129.7 11.1 %copy-start.6 = (bf16[128,640]{1,0:T(8,128)(2,1)S(1)}, bf16[128,640]{1,0:T(8,128)(2,1)}, u32[]{:S(2)}) copy-start(bf16[128,640]{1,0:T(8,128)(2,1)} %param.26) | copy-start | bytes 491524
  130.7 2.6 %copy-start.11 = (bf16[2,8,128,128]{3,2,1,0:T(8,128)(2,1)S(1)}, bf16[2,8,128,128]{3,2,1,0:T(8,128)(2,1)}, u32[]{:S(2)}) copy-start(bf16[2,8,128,128]{3,2,1,0:T(8,128)(2,1)} %get-tuple-element.195) | copy-start | bytes 1572868 | tf_op jit(solution)/shard_map/while
  130.7 2.6 %copy-start.12 = (bf16[1024,128]{1,0:T(8,128)(2,1)S(1)}, bf16[1024,128]{1,0:T(8,128)(2,1)}, u32[]{:S(2)}) copy-start(bf16[1024,128]{1,0:T(8,128)(2,1)} %get-tuple-element.198) | copy-start | bytes 786436 | tf_op jit(solution)/shard_map/while
  135.0 2.6 %copy-start.11 = (bf16[2,8,128,128]{3,2,1,0:T(8,128)(2,1)S(1)}, bf16[2,8,128,128]{3,2,1,0:T(8,128)(2,1)}, u32[]{:S(2)}) copy-start(bf16[2,8,128,128]{3,2,1,0:T(8,128)(2,1)} %get-tuple-element.195) | copy-start | bytes 1572868 | tf_op jit(solution)/shard_map/while
  135.0 2.6 %copy-start.12 = (bf16[1024,128]{1,0:T(8,128)(2,1)S(1)}, bf16[1024,128]{1,0:T(8,128)(2,1)}, u32[]{:S(2)}) copy-start(bf16[1024,128]{1,0:T(8,128)(2,1)} %get-tuple-element.198) | copy-start | bytes 786436 | tf_op jit(solution)/shard_map/while
  146.3 6.7 %copy-start.7 = (bf16[64,512]{1,0:T(8,128)(2,1)S(1)}, bf16[64,512]{1,0:T(8,128)(2,1)}, u32[]{:S(2)}) copy-start(bf16[64,512]{1,0:T(8,128)(2,1)} %param.24) | copy-start | bytes 196612
  146.3 6.8 %copy-start.2 = (bf16[64,128,64]{2,1,0:T(8,128)(2,1)S(1)}, bf16[64,128,64]{2,1,0:T(8,128)(2,1)}, u32[]{:S(2)}) copy-start(bf16[64,128,64]{2,1,0:T(8,128)(2,1)} %copy-done.1) | copy-start | bytes 3145732
  149.4 29.6 %all-to-all-start = ((bf16[2,32,4,16,128]{4,3,2,0,1:T(8,128)(2,1)}), bf16[2,32,4,16,128]{4,3,2,0,1:T(8,128)(2,1)}, u32[]{:S(2)}, u32[]{:S(2)}) async-start(bf16[2,32,4,16,128]{4,3,2,0,1:T(8,128)(2,1)} %copy.92), calls=%async_computation | async-start | bytes 2097152 | tf_op jit(solution)/shard_map/all_to_all | solution.py:152
  152.7 57.1 %all-reduce.2.cloned.1.call-start = ((), (), s32[]{:S(2)}) async-start(), calls=%async_computation.2 | async-start | bytes 2097152 | tf_op jit(solution)/shard_map/psum | solution.py:124
  184.7 10.5 %copy-start.8 = (bf16[256,64]{0,1:T(8,128)(2,1)S(1)}, bf16[256,64]{0,1:T(8,128)(2,1)}, u32[]{:S(2)}) copy-start(bf16[256,64]{0,1:T(8,128)(2,1)} %param.25) | copy-start | bytes 98308
  184.7 19.3 %copy-start.5 = (bf16[2048,128]{1,0:T(8,128)(2,1)S(1)}, bf16[2048,128]{1,0:T(8,128)(2,1)}, u32[]{:S(2)}) copy-start(bf16[2048,128]{1,0:T(8,128)(2,1)} %copy-done.4) | copy-start | bytes 1572868
  191.5 21.7 %all-to-all-start.1 = ((bf16[32,4,16,128]{3,2,1,0:T(8,128)(2,1)}), bf16[32,4,16,128]{3,2,1,0:T(8,128)(2,1)S(1)}, u32[]{:S(2)}, u32[]{:S(2)}) async-start(bf16[32,4,16,128]{3,2,1,0:T(8,128)(2,1)} %bitcast.34), calls=%async_computation.1 | async-start | bytes 1048576 | tf_op jit(solution)/shard_map/all_to_all | solution.py:156
  212.3 3.2 %copy-start.3 = (bf16[128,1024]{1,0:T(8,128)(2,1)S(1)}, bf16[128,1024]{1,0:T(8,128)(2,1)}, u32[]{:S(2)}) copy-start(bf16[128,1024]{1,0:T(8,128)(2,1)} %param.28) | copy-start | bytes 786436
  212.3 3.2 %copy-start.13 = (bf16[512,128]{1,0:T(8,128)(2,1)S(1)}, bf16[512,128]{1,0:T(8,128)(2,1)}, u32[]{:S(2)}) copy-start(bf16[512,128]{1,0:T(8,128)(2,1)} %param.29) | copy-start | bytes 393220
  (4 other events, 4.4 us)
Sparse Core Ops, SparseCore 0:
  160.9 48.8 all-reduce.1
